TPU v7x, 32 devices: a whole 2x2x4 slice. The times are simulated.
32 devices in a mesh: pole: 2 (over y), row: 4 (over z), col: 4 (over x, core).
Axes of the slice: x: 2, y: 2, z: 4, core: 2. Of those that a mesh axis runs over, the one named last changes fastest.
Arguments:
- root_inverse: float32 [16384, 8192], P(('pole', 'row'), 'col'), parts along dimension 0, may hold values from -6 to 6
- lower_one: float32 [16384, 512], P(('pole', 'row'), 'col'), parts along dimension 0, may hold values from -0.0625 to 0.0625
- pattern_one: int32 [64, 4], replicated, may hold values from 0 to 1, as said below
- diag_one: float32 [256, 512], P('pole', 'col'), parts along dimension 0, may hold values from -6 to 6
- lower_two: float32 [16384, 1024], P(('pole', 'row'), 'col'), parts along dimension 0, may hold values from -0.0625 to 0.0625
- pattern_two: int32 [64, 8], replicated, may hold values from 0 to 1, as said below
- parent_two: int32 [8], replicated, may hold values from 0 to 3, as said below
- lower_parent: float32 [256, 1024], P('pole', 'col'), parts along dimension 0, may hold values from -0.5 to 0.5
- diag_two: float32 [256, 1024], P('pole', 'col'), parts along dimension 0, may hold values from -6 to 6
Outputs:
- inverse_off_one: float32 [16384, 512], P(('pole', 'row'), 'col'), parts along dimension 0
- inverse_diagonal_first: float32 [256, 512], P('pole', 'col'), parts along dimension 0
- inverse_off_two: float32 [16384, 1024], P(('pole', 'row'), 'col'), parts along dimension 0
- inverse_parent_two: float32 [256, 1024], P('pole', 'col'), parts along dimension 0
- inverse_diag_two: float32 [256, 1024], P('pole', 'col'), parts along dimension 0
There are 2 independent parts, one for each index of `pole`. A program takes and returns all parts, laid end to end along the dimension named above; an argument that names none is the same for every part. Nothing has to cross between parts.
Inputs may be any that keep to these rules, and one draw needn't show every extreme that they name: pattern_one[i, k] is 1 where root block row i lies in the structure of first-level supernode k. `parent_two`: each first-level supernode is the parent of exactly two second-level supernodes. pattern_two[i, m] is 1 only where pattern_one[i, parent_two[m]] is 1.
All inputs are finite; a program needn't handle non-finite values.
Results may differ from a plain program's by a relative error of at most 0.000088.
Values sent between devices are 32-bit elements; how exact they have to be, the bound alone decides.
No kernel may reach another device: no remote copies, remote signals or barrier semaphores. Data moves between devices by JAX's collectives and lax.ppermute only.
A program may use at most 128 MiB of HBM per device.

v0:
```python
import jax
import jax.numpy as jnp
from jax import lax
from jax.sharding import PartitionSpec as P

BLOCK_SIDE = 128
PRECISION_MODE = lax.Precision.HIGHEST


def expand_blocks(pattern, block):
    count_rows, count_cols = pattern.shape
    spread = jnp.broadcast_to(
        pattern.astype(jnp.float32)[:, None, :, None], (count_rows, block, count_cols, block)
    )
    return spread.reshape(count_rows * block, count_cols * block)


def product(left_part, right_part):
    return jnp.dot(
        left_part, right_part, precision=PRECISION_MODE, preferred_element_type=jnp.float32
    )


def guarded(left_part, right_part):
    return product(left_part, right_part)


def block_inner(masked, solved):
    rows_here = masked.shape[0]
    blocks = masked.shape[1] // BLOCK_SIDE
    inner = jnp.einsum(
        "ikb,ikc->bkc",
        masked.reshape(rows_here, blocks, BLOCK_SIDE),
        solved.reshape(rows_here, blocks, BLOCK_SIDE),
        precision=PRECISION_MODE,
    )
    return inner.reshape(BLOCK_SIDE, blocks * BLOCK_SIDE)


def column_sums(partial_sum):
    return lax.psum_scatter(partial_sum, "col", scatter_dimension=1, tiled=True)


def block_totals(stacked):
    return lax.psum(stacked, "row")


def broadcast_product(root_block, masked):
    ranks_row = lax.axis_size("row")
    ranks_col = lax.axis_size("col")
    rows_here = root_block.shape[0]
    piece_width = masked.shape[1] // ranks_row
    swapped = lax.all_to_all(
        lax.all_to_all(masked, "row", split_axis=1, concat_axis=0, tiled=True),
        "col",
        split_axis=0,
        concat_axis=1,
        tiled=True,
    )
    gathered = guarded(root_block, lax.all_gather(swapped, "row", axis=1, tiled=True))
    ordered = gathered.reshape(rows_here, ranks_row, ranks_col, piece_width).transpose(0, 2, 1, 3)
    return ordered.reshape(rows_here, ranks_row * ranks_col * piece_width)


def local(
    root_inverse,
    lower_one,
    pattern_one,
    diag_one,
    lower_two,
    pattern_two,
    parent_two,
    lower_parent,
    diag_two,
):
    rows_here = root_inverse.shape[0]
    row_blocks = rows_here // BLOCK_SIDE
    row_start = lax.axis_index("row") * row_blocks
    col_index = lax.axis_index("col")
    col_one = lower_one.shape[1] // BLOCK_SIDE
    col_two = lower_two.shape[1] // BLOCK_SIDE
    first_supernodes = pattern_one.shape[1]
    super_two = pattern_two.shape[1]
    rows_one = lax.dynamic_slice_in_dim(pattern_one, row_start, row_blocks, 0)
    rows_two = lax.dynamic_slice_in_dim(pattern_two, row_start, row_blocks, 0)
    mask_one = expand_blocks(
        lax.dynamic_slice_in_dim(rows_one, col_index * col_one, col_one, 1), BLOCK_SIDE
    )
    mask_two = expand_blocks(
        lax.dynamic_slice_in_dim(rows_two, col_index * col_two, col_two, 1), BLOCK_SIDE
    )
    masked_one = lower_one * mask_one
    masked_two = lower_two * mask_two
    owned_parent = lax.dynamic_slice_in_dim(parent_two, col_index * col_two, col_two, 0)
    select_owned_blocks = (
        owned_parent[None, :] == jnp.arange(first_supernodes, dtype=jnp.int32)[:, None]
    ).astype(jnp.float32)
    link_own = lower_parent.reshape(BLOCK_SIDE, col_two, BLOCK_SIDE)
    solved_one = column_sums(broadcast_product(root_inverse, masked_one))
    inverse_off_one = -(mask_one * solved_one)
    inverse_diagonal_first = (
        diag_one + block_totals(jnp.stack([block_inner(masked_one, solved_one)]))[0]
    )
    rows_all, link_all, diagonal_blocks_full = (
        lax.all_gather(masked_two, "col", axis=1, tiled=True),
        lax.all_gather(lower_parent, "col", axis=1, tiled=True),
        lax.all_gather(inverse_diagonal_first, "col", axis=1, tiled=True),
    )
    local_ids = col_index * col_one + jnp.arange(col_one, dtype=jnp.int32)
    pick_all = (parent_two[None, :] == local_ids[:, None]).astype(jnp.float32)
    parent_cols = jnp.einsum(
        "ikb,km->imb",
        inverse_off_one.reshape(rows_here, col_one, BLOCK_SIDE),
        pick_all,
        precision=PRECISION_MODE,
    )
    direct = broadcast_product(root_inverse, masked_two)
    direct = direct + jnp.einsum(
        "imb,bme->ime",
        parent_cols,
        link_all.reshape(BLOCK_SIDE, super_two, BLOCK_SIDE),
        precision=PRECISION_MODE,
    ).reshape(rows_here, super_two * BLOCK_SIDE)
    across_all = jnp.einsum(
        "imb,ime->bme",
        parent_cols,
        rows_all.reshape(rows_here, super_two, BLOCK_SIDE),
        precision=PRECISION_MODE,
    ).reshape(BLOCK_SIDE, super_two * BLOCK_SIDE)
    summed = column_sums(jnp.concatenate([direct, across_all], axis=0))
    solved_two = summed[:rows_here]
    across_part = summed[rows_here:]
    totals = block_totals(jnp.stack([block_inner(masked_two, solved_two), across_part]))
    parent_diagonal = jnp.einsum(
        "vfl,fo->vol",
        diagonal_blocks_full.reshape(BLOCK_SIDE, first_supernodes, BLOCK_SIDE),
        select_owned_blocks,
        precision=PRECISION_MODE,
    )
    across = totals[1].reshape(BLOCK_SIDE, col_two, BLOCK_SIDE) + jnp.einsum(
        "bmd,dme->bme", parent_diagonal, link_own, precision=PRECISION_MODE
    )
    inverse_diag_two = (
        diag_two
        + totals[0]
        + jnp.einsum("dmb,dme->bme", link_own, across, precision=PRECISION_MODE).reshape(
            BLOCK_SIDE, col_two * BLOCK_SIDE
        )
    )
    return (
        inverse_off_one,
        inverse_diagonal_first,
        -(mask_two * solved_two),
        -across.reshape(BLOCK_SIDE, col_two * BLOCK_SIDE),
        inverse_diag_two,
    )


def solution(mesh):
    return jax.shard_map(
        local,
        mesh=mesh,
        in_specs=(
            P(("pole", "row"), "col"),
            P(("pole", "row"), "col"),
            P(),
            P("pole", "col"),
            P(("pole", "row"), "col"),
            P(),
            P(),
            P("pole", "col"),
            P("pole", "col"),
        ),
        out_specs=(
            P(("pole", "row"), "col"),
            P("pole", "col"),
            P(("pole", "row"), "col"),
            P("pole", "col"),
            P("pole", "col"),
        ),
        check_vma=False,
    )
```

profile of v0, /device:TPU:0, one launch (start us, length us, event | category | flops | bytes accessed | tf_op | source)
XLA Modules:
  0.0 674.4 jit_solution(6529609036820438768)
XLA Ops:
  7.2 1.6 copy.31
  8.8 0.8 convert_bitcast_fusion
  9.6 0.1 broadcast_multiply_fusion
  9.7 1.0 copy-done.3
  10.7 31.8 %all_to_all.64 = f32[2048,4,32]{0,2,1:T(8,128)S(1)} all-to-all(f32[2048,4,32]{0,2,1:T(8,128)S(1)} %bitcast.119), channel_id=1, replica_groups=mesh['pole'=2,'row'=4,'col'=4] {'row'}, dimensions={1} | all-to-all | bytes 2097152 | tf_op jit(solution)/shard_map/all_to_all | solution.py:54
  42.5 17.6 %all_to_all.65 = f32[4,2048,32]{1,2,0:T(8,128)} all-to-all(f32[4,2048,32]{1,2,0:T(8,128)S(1)} %bitcast.127), channel_id=1, replica_groups=mesh['pole'=2,'row'=4,'col'=4] {'col'}, dimensions={0} | all-to-all | bytes 2097152 | tf_op jit(solution)/shard_map/all_to_all | solution.py:53
  60.2 79.1 %all-gather.4.cloned.1.call-done = f32[2048,512]{0,1:T(8,128)} async-done(((f32[2048,128]{0,1:T(8,128)}), f32[2048,512]{0,1:T(8,128)}) %all-gather.4.cloned.1.call-update) | async-done | bytes 4194320 | tf_op jit(solution)/shard_map/all_gather | solution.py:60
  139.3 31.7 %fusion.26 = f32[512,2048]{1,0:T(8,128)S(1)} fusion(f32[2048,512]{0,1:T(8,128)} %all-gather.4.cloned.1.call-done, f32[2048,2048]{1,0:T(8,128)} %param.9), kind=kOutput, calls=%fused_computation.41 | convolution fusion | flops 25769803776 | bytes 25165824 | tf_op jit(solution)/shard_map/dot_general | solution.py:19
  170.9 2.2 copy.32
  173.2 1.9 copy.34
  175.2 0.8 dynamic-slice_convert_fusion
  175.9 0.2 broadcast_in_dim.25
  176.2 1.3 copy-done.1
  177.5 2.4 bitcast_multiply_fusion.1
  179.9 52.1 %all_to_all.66 = f32[2048,4,64]{0,2,1:T(8,128)S(1)} all-to-all(f32[2048,4,64]{0,2,1:T(8,128)} %bitcast.114), channel_id=1, replica_groups=mesh['pole'=2,'row'=4,'col'=4] {'row'}, dimensions={1} | all-to-all | bytes 4194304 | tf_op jit(solution)/shard_map/all_to_all | solution.py:54
  232.1 51.7 %all_to_all.67 = f32[4,2048,64]{1,2,0:T(8,128)} all-to-all(f32[4,2048,64]{1,2,0:T(8,128)S(1)} %bitcast.123), channel_id=1, replica_groups=mesh['pole'=2,'row'=4,'col'=4] {'col'}, dimensions={0} | all-to-all | bytes 4194304 | tf_op jit(solution)/shard_map/all_to_all | solution.py:53
  283.9 10.7 %all_gather.17 = f32[128,1024]{1,0:T(8,128)S(1)} all-gather(f32[128,256]{1,0:T(8,128)S(1)} %copy-done.5), channel_id=1, replica_groups=mesh['pole'=2,'row'=4,'col'=4] {'col'}, dimensions={1}, use_global_device_ids=true | all-gather | bytes 655360 | tf_op jit(solution)/shard_map/all_gather | solution.py:106
  294.5 0.2 copy.37
  294.8 1.3 multiply_negate_fusion
  296.1 0.3 copy.42
  296.5 10.4 %fusion.2 = f32[8,2048,128]{1,2,0:T(8,128)} fusion(f32[128,8,128]{0,2,1:T(8,128)S(1)} %bitcast.129, f32[2048,128]{1,0:T(8,128)S(1)} %copy.42, f32[8]{0:T(128)S(1)} %compare_convert_fusion), kind=kOutput, calls=%fused_computation.4 | convolution fusion | flops 3223322624 | bytes 9961504 | tf_op jit(solution)/shard_map/imb,bme->ime/dot_general | solution.py:118
  306.8 11.1 %fusion = f32[8,128,128]{2,1,0:T(8,128)S(1)} fusion(f32[2048,8,128]{0,2,1:T(8,128)} %bitcast.120, f32[2048,128]{1,0:T(8,128)S(1)} %copy.42, f32[8]{0:T(128)S(1)} %compare_convert_fusion), kind=kOutput, calls=%fused_computation.2 | convolution fusion | flops 3223322624 | bytes 9961504 | tf_op jit(solution)/shard_map/imb,ime->bme/dot_general | solution.py:124
  317.9 135.5 %all-gather.6.cloned.1.call-done = f32[2048,1024]{0,1:T(8,128)} async-done(((f32[2048,256]{0,1:T(8,128)}), f32[2048,1024]{0,1:T(8,128)}) %all-gather.6.cloned.1.call-update) | async-done | bytes 8388624 | tf_op jit(solution)/shard_map/all_gather | solution.py:60
  453.4 60.4 %fusion.27 = f32[1024,2048]{1,0:T(8,128)S(1)} fusion(f32[2048,1024]{0,1:T(8,128)} %all-gather.6.cloned.1.call-done, f32[2048,2048]{1,0:T(8,128)} %param.9), kind=kOutput, calls=%fused_computation.42 | convolution fusion | flops 51539607552 | bytes 33554432 | tf_op jit(solution)/shard_map/dot_general | solution.py:19
  513.8 3.9 copy.35
  517.7 11.8 %bitcast_add_fusion = f32[2048,1024]{0,1:T(8,128)} fusion(f32[8,2048,128]{1,2,0:T(8,128)} %fusion.2, f32[2048,4,4,64]{0,3,1,2:T(8,128)} %copy.35), kind=kLoop, calls=%fused_computation.1 | loop fusion | flops 2097152 | bytes 25165824 | tf_op jit(solution)/shard_map/add | solution.py:118
  529.4 7.6 %pad_maximum_fusion = f32[2176,1024]{0,1:T(8,128)} fusion(f32[128,1024]{0,1:T(8,128)S(1)} %bitcast.128, f32[2048,1024]{0,1:T(8,128)} %bitcast_add_fusion), kind=kLoop, calls=%fused_computation | loop fusion | flops 2228224 | bytes 17825792 | tf_op jit(solution)/shard_map/concatenate | solution.py:130
  537.1 1.1 copy-done.4
  538.2 2.9 convolution_bitcast_fusion.1
  541.1 69.4 %reduce-scatter.5.cloned.1.call-done = f32[2176,256]{0,1:T(8,128)} async-done(((f32[2176,1024]{0,1:T(8,128)}), f32[2176,256]{0,1:T(8,128)}) %reduce-scatter.5.cloned.1.call-update) | async-done | bytes 2228240 | tf_op jit(solution)/shard_map/reduce_scatter | solution.py:41
  610.5 4.7 fusion.10
  615.2 2.0 fusion.28
  617.2 0.9 slice_bitcast_fusion.1
  618.1 0.7 pad_maximum_fusion.1
  619.1 0.1 copy.40
  619.2 2.9 copy.44
  622.0 33.3 %all-reduce.3.cloned.1.call-done = (f32[128,128]{0,1:T(8,128)}, f32[2,128,256]{1,2,0:T(8,128)}) async-done(((f32[128,128]{0,1:T(8,128)}, f32[2,128,256]{1,2,0:T(8,128)}), (f32[128,128]{0,1:T(8,128)}, f32[2,128,256]{1,2,0:T(8,128)})) %all-reduce.3.cloned.1.call-update) | async-done | bytes 327696 | tf_op jit(solution)/shard_map/psum | solution.py:45
  655.4 0.8 add.40
  656.2 0.7 copy.43
  657.0 5.8 all_gather.19
  662.7 0.9 slice.18
  663.6 0.1 copy.48
  663.8 0.4 fusion.22
  664.2 0.4 fusion.25
  664.6 0.8 copy.45
  665.4 0.3 fusion.13
  665.7 0.9 fusion.16
  666.6 0.8 copy.46
  (33 shorter events, 0.6 us)
Async XLA Ops:
  7.2 132.1 %all-gather.4.cloned.1.call-start = ((), (), s32[]{:S(2)}) async-start(), calls=%async_computation.6 | async-start | bytes 5242880 | tf_op jit(solution)/shard_map/all_gather | solution.py:60
  9.7 1.0 copy-start.3
  60.2 234.6 %reduce-scatter.3.cloned.1.call-start = ((), (), s32[]{:S(2)}) async-start(), calls=%async_computation.7 | async-start | bytes 5242880 | tf_op jit(solution)/shard_map/reduce_scatter | solution.py:41
  173.2 133.6 %all-gather.8.cloned.1.call-start = ((), (), s32[]{:S(2)}) async-start(), calls=%async_computation.9 | async-start | bytes 10485760 | tf_op jit(solution)/shard_map/all_gather | solution.py:105
  176.2 1.3 copy-start.1
  177.5 106.4 %copy-start.5 = (f32[128,256]{1,0:T(8,128)S(1)}, f32[128,256]{1,0:T(8,128)}, u32[]{:S(2)}) copy-start(f32[128,256]{1,0:T(8,128)} %param.16) | copy-start | bytes 393220
  179.9 114.9 %copy-start.8 = (s32[8]{0:T(128)S(1)}, s32[8]{0:T(128)}, u32[]{:S(2)}) copy-start(s32[8]{0:T(128)} %param.15) | copy-start | bytes 100
  179.9 273.5 %all-gather.6.cloned.1.call-start = ((), (), s32[]{:S(2)}) async-start(), calls=%async_computation.8 | async-start | bytes 10485760 | tf_op jit(solution)/shard_map/all_gather | solution.py:60
  283.8 326.7 %reduce-scatter.5.cloned.1.call-start = ((), (), s32[]{:S(2)}) async-start(), calls=%async_computation.10 | async-start | bytes 11141120 | tf_op jit(solution)/shard_map/reduce_scatter | solution.py:41
  296.4 21.5 %copy-start.2 = (f32[2048,128]{1,0:T(8,128)}, f32[2048,128]{1,0:T(8,128)S(1)}, u32[]{:S(2)}) copy-start(f32[2048,128]{1,0:T(8,128)S(1)} %copy.42) | copy-start | bytes 3145732
  537.0 1.2 copy-start.4
  537.0 78.2 %copy-start = (f32[2048,256]{0,1:T(8,128)S(1)}, f32[2048,256]{0,1:T(8,128)}, u32[]{:S(2)}) copy-start(f32[2048,256]{0,1:T(8,128)} %bitcast_multiply_fusion.1) | copy-start | bytes 6291460
  537.0 81.9 %copy-start.7 = (f32[128,128]{1,0:T(8,128)S(1)}, f32[128,128]{1,0:T(8,128)}, u32[]{:S(2)}) copy-start(f32[128,128]{1,0:T(8,128)} %param.12) | copy-start | bytes 196612
  537.0 82.0 %copy-start.6 = (f32[128,256]{1,0:T(8,128)S(1)}, f32[128,256]{1,0:T(8,128)}, u32[]{:S(2)}) copy-start(f32[128,256]{1,0:T(8,128)} %param.17) | copy-start | bytes 393220
  537.0 118.3 %all-reduce.3.cloned.1.call-start = ((), (), s32[]{:S(2)}) async-start(), calls=%async_computation.11 | async-start | bytes 655360 | tf_op jit(solution)/shard_map/psum | solution.py:45
Sparse Core Ops, SparseCore 0:
  60.3 78.9 all-gather.3
  173.3 43.0 reduce-scatter.2
  218.6 83.5 all-gather.7
  303.7 149.6 all-gather.5
  537.1 73.2 reduce-scatter.4
  619.0 36.3 all-reduce.2
where the time goes:
time: 683 us; the launch traced here: 674 us
  waiting for transfers between devices  317 us (46%)
  blocking collectives  170 us (25%)
  matrix products  120 us (18%)
  other arithmetic  31.8 us (5%)
  local copies, waits for them, and re-layouts  21.2 us (3%)
  between operations  14.6 us (2%)
    all_gather x2, waiting for transfers between devices, broadcast_product(): lax.all_gather(swapped, 'row', axis=1, tiled=True)  215 us
    dot_general x2, matrix products, product(): jnp.dot(left_part, right_part, precision=PRECISION_MODE, preferred_elemen...  92.1 us
    all_to_all x2, blocking collectives, broadcast_product(): lax.all_to_all(masked, 'row', split_axis=1, concat_axis=0, tiled=True)  83.9 us
    reduce_scatter x2, waiting for transfers between devices, column_sums(): return lax.psum_scatter(partial_sum, 'col', scatter_dimension=1, tiled=True)  69.4 us
    all_to_all x2, blocking collectives, broadcast_product(): lax.all_to_all(lax.all_to_all(masked, 'row', split_axis=1, concat_axis=0,...  69.3 us
    psum x1, waiting for transfers between devices, block_totals(): return lax.psum(stacked, 'row')  33.3 us
  transfers between devices with their start and end apart: 6, of which 4 were waited for; matrix products, arithmetic and copies ran while one was open for 5% of the time, Pallas kernels for 0%

commit v1 on v0

--- a/solution.py
+++ b/solution.py
@@ -50,13 +50,16 @@
     ranks_col = lax.axis_size("col")
     rows_here = root_block.shape[0]
     piece_width = masked.shape[1] // ranks_row
-    swapped = lax.all_to_all(
-        lax.all_to_all(masked, "row", split_axis=1, concat_axis=0, tiled=True),
-        "col",
-        split_axis=0,
-        concat_axis=1,
-        tiled=True,
-    )
+    shard = lax.all_to_all(masked, "row", split_axis=1, concat_axis=0, tiled=True)
+    ways, here = (lax.axis_size("col"), lax.axis_index("col"))
+    width = shard.shape[0] // ways
+    turned = jnp.roll(shard, -here * width, axis=0)
+    got = [lax.slice_in_dim(turned, 0, width, axis=0)]
+    for far in range(1, ways):
+        sent = lax.slice_in_dim(turned, far * width, (far + 1) * width, axis=0)
+        got.append(lax.ppermute(sent, "col", [(d, (d + far) % ways) for d in range(ways)]))
+    line = jnp.concatenate(got[::-1], axis=1)
+    swapped = jnp.roll(line, (here + 1) * got[0].shape[1], axis=1)
     gathered = guarded(root_block, lax.all_gather(swapped, "row", axis=1, tiled=True))
     ordered = gathered.reshape(rows_here, ranks_row, ranks_col, piece_width).transpose(0, 2, 1, 3)
     return ordered.reshape(rows_here, ranks_row * ranks_col * piece_width)

time: 683 us -> 619 us (0.906)
  blocking collectives: 170 us -> 13.8 us
  waiting for transfers between devices: 317 us -> 381 us
  local copies, waits for them, and re-layouts: 21.2 us -> 35.4 us
  starting transfers between devices: 0.25 us -> 13.6 us
    all_to_all x4 -> x0, blocking collectives: 153 us -> none  [the longest x2 83.9 us: broadcast_product(): lax.all_to_all(masked, 'row', split_axis=1, concat_axis=0, tiled=True)]
    all_gather x2, waiting for transfers between devices: 215 us -> 105 us  [broadcast_product(): lax.all_gather(swapped, 'row', axis=1, tiled=True)]
    all_to_all x0 -> x2, waiting for transfers between devices: none -> 105 us  [broadcast_product(): lax.all_to_all(masked, 'row', split_axis=1, concat_axis=0, tiled=True)]
    all_gather x1, waiting for transfers between devices: 0.01 us -> 37.3 us  [local(): lax.all_gather(masked_two, 'col', axis=1, tiled=True)]
    ppermute x0 -> x6, waiting for transfers between devices: none -> 27.9 us  [broadcast_product(): lax.ppermute(sent, 'col', [(d, (d + far) % ways) for d in range(ways)])]
    all_to_all x0 -> x2, starting transfers between devices: none -> 10.8 us  [broadcast_product(): lax.all_to_all(masked, 'row', split_axis=1, concat_axis=0, tiled=True)]
    unnamed x27 -> x43, local copies, waits for them, and re-layouts: 12.5 us -> 18.4 us
  transfers between devices with their start and end apart: 6 -> 14, of which waited for: 4 -> 10; matrix products, arithmetic and copies ran while one was open for 5% -> 21% of each run, Pallas kernels for 0% -> 0%
where the time goes in v1:
time: 619 us; the launch traced here: 614 us
  waiting for transfers between devices  381 us (62%)
  matrix products  122 us (20%)
  local copies, waits for them, and re-layouts  35.4 us (6%)
  other arithmetic  33.9 us (5%)
  between operations  14.7 us (2%)
  blocking collectives  13.8 us (2%)
  starting transfers between devices  13.6 us (2%)
    all_gather x2, waiting for transfers between devices, broadcast_product(): lax.all_gather(swapped, 'row', axis=1, tiled=True)  105 us
    all_to_all x2, waiting for transfers between devices, broadcast_product(): lax.all_to_all(masked, 'row', split_axis=1, concat_axis=0, tiled=True)  105 us
    dot_general x2, matrix products, product(): jnp.dot(left_part, right_part, precision=PRECISION_MODE, preferred_elemen...  92.4 us
    reduce_scatter x2, waiting for transfers between devices, column_sums(): return lax.psum_scatter(partial_sum, 'col', scatter_dimension=1, tiled=True)  71.2 us
    all_gather x1, waiting for transfers between devices, local(): lax.all_gather(masked_two, 'col', axis=1, tiled=True)  37.3 us
    psum x1, waiting for transfers between devices, block_totals(): return lax.psum(stacked, 'row')  34.4 us
    ppermute x6, waiting for transfers between devices, broadcast_product(): lax.ppermute(sent, 'col', [(d, (d + far) % ways) for d in range(ways)])  27.9 us
    unnamed x43, local copies, waits for them, and re-layouts  18.4 us
  transfers between devices with their start and end apart: 14, of which 10 were waited for; matrix products, arithmetic and copies ran while one was open for 21% of the time, Pallas kernels for 0%

profile of v1, /device:TPU:0, one launch (start us, length us, event | category | flops | bytes accessed | tf_op | source)
XLA Modules:
  0.0 614.0 jit_solution(16063083499092260409)
XLA Ops:
  7.2 1.6 copy.31
  9.6 1.1 broadcast_multiply_fusion
  10.6 6.3 %all-to-all-start = ((f32[2048,4,32]{0,2,1:T(8,128)}), f32[2048,4,32]{0,2,1:T(8,128)S(1)}, u32[]{:S(2)}, u32[]{:S(2)}) async-start(f32[2048,4,32]{0,2,1:T(8,128)} %bitcast.2), calls=%async_computation | async-start | bytes 2097152 | tf_op jit(solution)/shard_map/all_to_all | solution.py:53
  17.0 2.9 copy.35
  20.6 22.1 %all-to-all-done = f32[2048,4,32]{0,2,1:T(8,128)S(1)} async-done(((f32[2048,4,32]{0,2,1:T(8,128)}), f32[2048,4,32]{0,2,1:T(8,128)S(1)}, u32[]{:S(2)}, u32[]{:S(2)}) %all-to-all-start) | async-done | bytes 1048608 | tf_op jit(solution)/shard_map/all_to_all | solution.py:53
  43.0 0.9 fusion.28
  44.1 1.3 collective-permute-start.1
  45.6 2.4 bitcast_multiply_fusion.1
  48.0 4.4 all-to-all-start.1
  52.8 2.9 collective-permute-done.1
  55.7 1.0 constant_dynamic-update-slice_fusion.4
  56.7 1.9 collective-permute-done.2
  58.7 1.0 constant_dynamic-update-slice_fusion.1
  59.7 1.1 constant_dynamic-slice_fusion.1
  60.8 82.5 %all-to-all-done.1 = f32[2048,4,64]{0,2,1:T(8,128)} async-done(((f32[2048,4,64]{0,2,1:T(8,128)}), f32[2048,4,64]{0,2,1:T(8,128)}, u32[]{:S(2)}, u32[]{:S(2)}) %all-to-all-start.1) | async-done | bytes 2097184 | tf_op jit(solution)/shard_map/all_to_all | solution.py:53
  143.3 1.7 copy.54
  145.5 1.3 copy-done
  146.9 1.2 fusion.27
  148.5 12.1 %collective-permute-done.3 = f32[2048,64]{0,1:T(8,128)S(1)} collective-permute-done((f32[2048,64]{0,1:T(8,128)}, f32[2048,64]{0,1:T(8,128)S(1)}, u32[]{:S(2)}, u32[]{:S(2)}) %collective-permute-start.3) | collective-permute-done | bytes 524320 | tf_op jit(solution)/shard_map/ppermute | solution.py:60
  160.7 11.0 %collective-permute-done.4 = f32[2048,64]{0,1:T(8,128)S(1)} collective-permute-done((f32[2048,64]{0,1:T(8,128)}, f32[2048,64]{0,1:T(8,128)S(1)}, u32[]{:S(2)}, u32[]{:S(2)}) %collective-permute-start.4) | collective-permute-done | bytes 524320 | tf_op jit(solution)/shard_map/ppermute | solution.py:60
  171.8 1.1 constant_dynamic-update-slice_fusion.9
  172.8 1.1 slice_dynamic-update-slice_fusion
  174.0 1.1 constant_dynamic-update-slice_fusion.6
  175.1 1.1 slice_dynamic-update-slice_fusion.1
  176.2 1.5 constant_dynamic-slice_fusion
  178.1 31.7 %fusion.30 = f32[512,2048]{1,0:T(8,128)S(1)} fusion(f32[2048,512]{0,1:T(8,128)} %all-gather.4.cloned.1.call-done, f32[2048,2048]{1,0:T(8,128)} %param.9), kind=kOutput, calls=%fused_computation.67 | convolution fusion | flops 25769803776 | bytes 25165824 | tf_op jit(solution)/shard_map/dot_general | solution.py:19
  209.8 2.2 copy.33
  212.9 8.0 %all_gather.17 = f32[128,1024]{1,0:T(8,128)S(1)} all-gather(f32[128,256]{1,0:T(8,128)S(1)} %copy-done.6), channel_id=1, replica_groups=mesh['pole'=2,'row'=4,'col'=4] {'col'}, dimensions={1}, use_global_device_ids=true | all-gather | bytes 655360 | tf_op jit(solution)/shard_map/all_gather | solution.py:109
  221.0 1.0 copy.39
  222.0 104.7 %all-gather.6.cloned.1.call-done = f32[2048,1024]{0,1:T(8,128)} async-done(((f32[2048,256]{0,1:T(8,128)}), f32[2048,1024]{0,1:T(8,128)}) %all-gather.6.cloned.1.call-update) | async-done | bytes 8388624 | tf_op jit(solution)/shard_map/all_gather | solution.py:63
  326.7 60.7 %fusion.31 = f32[1024,2048]{1,0:T(8,128)S(1)} fusion(f32[2048,1024]{0,1:T(8,128)} %all-gather.6.cloned.1.call-done, f32[2048,2048]{1,0:T(8,128)} %param.9), kind=kOutput, calls=%fused_computation.68 | convolution fusion | flops 51539607552 | bytes 33554432 | tf_op jit(solution)/shard_map/dot_general | solution.py:19
  387.4 3.8 copy.37
  391.2 2.3 multiply_negate_fusion
  393.5 1.5 copy.44
  395.1 37.3 %all-gather.8.cloned.1.call-done = f32[2048,1024]{0,1:T(8,128)} async-done(((f32[2048,256]{0,1:T(8,128)}), f32[2048,1024]{0,1:T(8,128)}) %all-gather.8.cloned.1.call-update) | async-done | bytes 8388624 | tf_op jit(solution)/shard_map/all_gather | solution.py:108
  432.4 11.3 %fusion = f32[8,128,128]{2,1,0:T(8,128)S(1)} fusion(f32[2048,8,128]{0,2,1:T(8,128)} %bitcast.115, f32[2048,128]{1,0:T(8,128)S(1)} %copy.44, f32[8]{0:T(128)S(1)} %compare_convert_fusion), kind=kOutput, calls=%fused_computation.2 | convolution fusion | flops 3223322624 | bytes 9961504 | tf_op jit(solution)/shard_map/imb,ime->bme/dot_general | solution.py:127
  443.7 10.5 %fusion.2 = f32[8,2048,128]{1,2,0:T(8,128)} fusion(f32[128,8,128]{0,2,1:T(8,128)S(1)} %bitcast.123, f32[2048,128]{1,0:T(8,128)S(1)} %copy.44, f32[8]{0:T(128)S(1)} %compare_convert_fusion), kind=kOutput, calls=%fused_computation.4 | convolution fusion | flops 3223322624 | bytes 9961504 | tf_op jit(solution)/shard_map/imb,bme->ime/dot_general | solution.py:121
  454.3 11.8 %bitcast_add_fusion = f32[2048,1024]{0,1:T(8,128)} fusion(f32[8,2048,128]{1,2,0:T(8,128)} %fusion.2, f32[2048,4,4,64]{0,3,1,2:T(8,128)} %copy.37), kind=kLoop, calls=%fused_computation.1 | loop fusion | flops 2097152 | bytes 25165824 | tf_op jit(solution)/shard_map/add | solution.py:121
  466.1 7.6 %pad_maximum_fusion = f32[2176,1024]{0,1:T(8,128)} fusion(f32[128,1024]{0,1:T(8,128)S(1)} %bitcast.122, f32[2048,1024]{0,1:T(8,128)} %bitcast_add_fusion), kind=kLoop, calls=%fused_computation | loop fusion | flops 2228224 | bytes 17825792 | tf_op jit(solution)/shard_map/concatenate | solution.py:133
  473.7 1.1 copy-done.4
  474.9 2.9 convolution_bitcast_fusion.1
  477.7 71.2 %reduce-scatter.5.cloned.1.call-done = f32[2176,256]{0,1:T(8,128)} async-done(((f32[2176,1024]{0,1:T(8,128)}), f32[2176,256]{0,1:T(8,128)}) %reduce-scatter.5.cloned.1.call-update) | async-done | bytes 2228240 | tf_op jit(solution)/shard_map/reduce_scatter | solution.py:41
  548.9 4.1 fusion.11
  553.0 3.8 fusion.32
  558.8 1.8 copy.46
  560.6 34.4 %all-reduce.3.cloned.1.call-done = (f32[128,128]{0,1:T(8,128)}, f32[2,128,256]{1,2,0:T(8,128)}) async-done(((f32[128,128]{0,1:T(8,128)}, f32[2,128,256]{1,2,0:T(8,128)}), (f32[128,128]{0,1:T(8,128)}, f32[2,128,256]{1,2,0:T(8,128)})) %all-reduce.3.cloned.1.call-update) | async-done | bytes 327696 | tf_op jit(solution)/shard_map/psum | solution.py:45
  596.6 5.8 all_gather.19
  605.3 0.9 fusion.18
  (71 shorter events, 12.3 us)
Async XLA Ops:
  10.6 32.0 %all-to-all-start = ((f32[2048,4,32]{0,2,1:T(8,128)}), f32[2048,4,32]{0,2,1:T(8,128)S(1)}, u32[]{:S(2)}, u32[]{:S(2)}) async-start(f32[2048,4,32]{0,2,1:T(8,128)} %bitcast.2), calls=%async_computation | async-start | bytes 2097152 | tf_op jit(solution)/shard_map/all_to_all | solution.py:53
  42.7 2.9 copy-start.2
  43.9 8.9 %collective-permute-start = (f32[2048,32]{0,1:T(8,128)}, f32[2048,32]{0,1:T(8,128)S(1)}, u32[]{:S(2)}, u32[]{:S(2)}) collective-permute-start(f32[2048,32]{0,1:T(8,128)} %get-tuple-element.24), channel_id=1, source_target_pairs={{0,3},{1,0},{2,1},{3,2},{4,7},{5,4},{6,5},{7,6},{8,11},{9,8},{10,9... | collective-permute-start | bytes 786440 | tf_op jit(solution)/shard_map/ppermute | solution.py:60
  44.1 11.6 %collective-permute-start.1 = (f32[2048,32]{0,1:T(8,128)}, f32[2048,32]{0,1:T(8,128)}, u32[]{:S(2)}, u32[]{:S(2)}) collective-permute-start(f32[2048,32]{0,1:T(8,128)} %get-tuple-element.23), channel_id=1, source_target_pairs={{0,2},{1,3},{2,0},{3,1},{4,6},{5,7},{6,4},{7,5},{8,10},{9,11},{10,... | collective-permute-start | bytes 786440 | tf_op jit(solution)/shard_map/ppermute | solution.py:60
  48.0 95.3 %all-to-all-start.1 = ((f32[2048,4,64]{0,2,1:T(8,128)}), f32[2048,4,64]{0,2,1:T(8,128)}, u32[]{:S(2)}, u32[]{:S(2)}) async-start(f32[2048,4,64]{0,2,1:T(8,128)} %bitcast.11), calls=%async_computation.2 | async-start | bytes 4194304 | tf_op jit(solution)/shard_map/all_to_all | solution.py:53
  52.5 125.6 %all-gather.4.cloned.1.call-start = ((), (), s32[]{:S(2)}) async-start(), calls=%async_computation.4 | async-start | bytes 5242880 | tf_op jit(solution)/shard_map/all_gather | solution.py:63
  52.5 6.1 collective-permute-start.2
  60.8 265.9 %all-gather.6.cloned.1.call-start = ((), (), s32[]{:S(2)}) async-start(), calls=%async_computation.6 | async-start | bytes 10485760 | tf_op jit(solution)/shard_map/all_gather | solution.py:63
  145.5 1.3 copy-start
  148.0 12.6 %collective-permute-start.3 = (f32[2048,64]{0,1:T(8,128)}, f32[2048,64]{0,1:T(8,128)S(1)}, u32[]{:S(2)}, u32[]{:S(2)}) collective-permute-start(f32[2048,64]{0,1:T(8,128)} %get-tuple-element.21), channel_id=1, source_target_pairs={{0,3},{1,0},{2,1},{3,2},{4,7},{5,4},{6,5},{7,6},{8,11},{9,8},{10,9... | collective-permute-start | bytes 1572872 | tf_op jit(solution)/shard_map/ppermute | solution.py:60
  148.0 23.7 %collective-permute-start.4 = (f32[2048,64]{0,1:T(8,128)}, f32[2048,64]{0,1:T(8,128)S(1)}, u32[]{:S(2)}, u32[]{:S(2)}) collective-permute-start(f32[2048,64]{0,1:T(8,128)} %get-tuple-element.20), channel_id=1, source_target_pairs={{0,2},{1,3},{2,0},{3,1},{4,6},{5,7},{6,4},{7,5},{8,10},{9,11},{10,... | collective-permute-start | bytes 1572872 | tf_op jit(solution)/shard_map/ppermute | solution.py:60
  148.0 23.7 %collective-permute-start.5 = (f32[2048,64]{0,1:T(8,128)}, f32[2048,64]{0,1:T(8,128)}, u32[]{:S(2)}, u32[]{:S(2)}) collective-permute-start(f32[2048,64]{0,1:T(8,128)} %get-tuple-element.19), channel_id=1, source_target_pairs={{0,1},{1,2},{2,3},{3,0},{4,5},{5,6},{6,7},{7,4},{8,9},{9,10},{10,1... | collective-permute-start | bytes 1572872 | tf_op jit(solution)/shard_map/ppermute | solution.py:60
  177.7 213.5 %reduce-scatter.3.cloned.1.call-start = ((), (), s32[]{:S(2)}) async-start(), calls=%async_computation.5 | async-start | bytes 5242880 | tf_op jit(solution)/shard_map/reduce_scatter | solution.py:41
  212.0 0.9 copy-start.6
  212.0 10.0 %copy-start.9 = (s32[8]{0:T(128)S(1)}, s32[8]{0:T(128)}, u32[]{:S(2)}) copy-start(s32[8]{0:T(128)} %param.15) | copy-start | bytes 100
  212.1 220.3 %all-gather.8.cloned.1.call-start = ((), (), s32[]{:S(2)}) async-start(), calls=%async_computation.7 | async-start | bytes 10485760 | tf_op jit(solution)/shard_map/all_gather | solution.py:108
  212.6 336.3 %reduce-scatter.5.cloned.1.call-start = ((), (), s32[]{:S(2)}) async-start(), calls=%async_computation.8 | async-start | bytes 11141120 | tf_op jit(solution)/shard_map/reduce_scatter | solution.py:41
  395.1 48.6 %copy-start.1 = (f32[2048,128]{1,0:T(8,128)}, f32[2048,128]{1,0:T(8,128)S(1)}, u32[]{:S(2)}) copy-start(f32[2048,128]{1,0:T(8,128)S(1)} %copy.44) | copy-start | bytes 3145732
  432.4 11.3 %copy-start.5 = (f32[128,1024]{0,1:T(8,128)S(1)}, f32[128,1024]{0,1:T(8,128)}, u32[]{:S(2)}) copy-start(f32[128,1024]{0,1:T(8,128)} %copy.39) | copy-start | bytes 1572868
  473.6 1.2 copy-start.4
  473.7 121.3 %all-reduce.3.cloned.1.call-start = ((), (), s32[]{:S(2)}) async-start(), calls=%async_computation.9 | async-start | bytes 655360 | tf_op jit(solution)/shard_map/psum | solution.py:45
  553.0 5.6 copy-start.8
  553.0 5.7 copy-start.7
  553.0 5.8 copy-start.3
Sparse Core Ops, SparseCore 0:
  60.9 108.1 all-gather.3
  177.9 148.7 all-gather.5
  329.2 42.7 reduce-scatter.2
  374.1 58.2 all-gather.7
  473.8 75.0 reduce-scatter.4
  558.6 36.3 all-reduce.2
